TPU v7x, 128 devices: a whole 4x4x4 slice. The times are simulated.
128 devices in a mesh: pipe: 8 (over x, z_hi), tensor: 16 (over z_lo, y, core).
Axes of the slice: x: 4, y: 4, z: 4 (z_hi: 2, z_lo: 2; z = z_hi * 2 + z_lo), core: 2. Of those that a mesh axis runs over, the one named last changes fastest.
Arguments:
- layer_input: bfloat16 [768, 8192], P('tensor', 'pipe'), may hold values from -6 to 6
- out_grad: bfloat16 [768, 8192], P('tensor', 'pipe'), may hold values from -2 to 2
- gate_pre: bfloat16 [768, 28672], P(None, 'tensor'), may hold values from -8 to 8
- up_pre: bfloat16 [768, 28672], P(None, 'tensor'), may hold values from -6 to 6
- gate_weight: bfloat16 [8192, 28672], P('pipe', 'tensor'), may hold values from -0.0625 to 0.0625
- up_weight: bfloat16 [8192, 28672], P('pipe', 'tensor'), may hold values from -0.0625 to 0.0625
- down_weight: bfloat16 [28672, 8192], P('tensor', 'pipe'), may hold values from -0.03125 to 0.03125
- gate_mask: int32 [64, 224], P('pipe', 'tensor'), may hold values from 0 to 1, as said below
- up_mask: int32 [64, 224], P('pipe', 'tensor'), may hold values from 0 to 1, as said below
- down_mask: int32 [224, 64], P('tensor', 'pipe'), may hold values from 0 to 1, as said below
Outputs:
- grad_input: bfloat16 [768, 8192], P('tensor', 'pipe')
- grad_gate: bfloat16 [8192, 28672], P('pipe', 'tensor')
- grad_up: bfloat16 [8192, 28672], P('pipe', 'tensor')
- grad_down: bfloat16 [28672, 8192], P('tensor', 'pipe')
Inputs may be any that keep to these rules, and one draw needn't show every extreme that they name: `gate_mask`: each entry is 1 for a kept block and 0 for a pruned one; the share of kept blocks differs from block column to block column. `up_mask`: each entry is 1 for a kept block and 0 for a pruned one; the share of kept blocks differs from block column to block column. `down_mask`: each entry is 1 for a kept block and 0 for a pruned one; the share of kept blocks differs from block row to block row.
All inputs are finite; a program needn't handle non-finite values.
Results may differ from a plain program's by a relative error of at most 0.005.
Values may be sent and summed in bfloat16 or wider, within the bound.
A program may use at most 128 MiB of HBM per device.

v0:
```python
import jax
import jax.numpy as jnp
from jax import lax
from jax.sharding import PartitionSpec as P

BLOCK = 128


def expand(mask):
    return jnp.repeat(jnp.repeat(mask, BLOCK, axis=0), BLOCK, axis=1)


def local_grads(hidden_grad, gate_val, up_val, sigma_val):
    gate_grad = (hidden_grad * up_val * sigma_val * (1.0 + gate_val * (1.0 - sigma_val))).astype(
        jnp.bfloat16
    )
    up_grad = (hidden_grad * gate_val * sigma_val).astype(jnp.bfloat16)
    return (gate_grad, up_grad)


def shards(
    layer_input,
    out_grad,
    gate_pre,
    up_pre,
    gate_weight,
    up_weight,
    down_weight,
    gate_mask,
    up_mask,
    down_mask,
):
    mask_gate = expand(gate_mask)
    mask_up = expand(up_mask)
    mask_down = expand(down_mask)
    gate_masked = gate_weight * mask_gate.astype(jnp.bfloat16)
    up_masked = up_weight * mask_up.astype(jnp.bfloat16)
    down_masked = down_weight * mask_down.astype(jnp.bfloat16)
    gate_val = gate_pre.astype(jnp.float32)
    up_val = up_pre.astype(jnp.float32)
    sigma_val = jax.nn.sigmoid(gate_val)
    hidden = (gate_val * sigma_val * up_val).astype(jnp.bfloat16)
    piece = lax.all_gather(out_grad, "tensor", axis=0, tiled=True)
    down_acc = lax.dot_general(
        hidden, piece, (((0,), (0,)), ((), ())), preferred_element_type=jnp.float32
    )
    partial_rows = lax.dot_general(
        piece, down_masked, (((1,), (1,)), ((), ())), preferred_element_type=jnp.float32
    )
    hidden_grad = partial_rows
    down_acc, hidden_partial = (down_acc, hidden_grad)
    grad_down = (down_acc * mask_down.astype(jnp.float32)).astype(jnp.bfloat16)
    hidden_grad = lax.psum(hidden_partial, "pipe")
    gate_grad, up_grad = local_grads(hidden_grad, gate_val, up_val, sigma_val)
    piece = lax.all_gather(layer_input, "tensor", axis=0, tiled=True)
    gate_rows = gate_grad
    up_rows = up_grad
    gate_acc = lax.dot_general(
        piece, gate_rows, (((0,), (0,)), ((), ())), preferred_element_type=jnp.float32
    )
    up_acc = lax.dot_general(
        piece, up_rows, (((0,), (0,)), ((), ())), preferred_element_type=jnp.float32
    )
    gate_acc, up_acc = (gate_acc, up_acc)
    grad_gate = (gate_acc * mask_gate.astype(jnp.float32)).astype(jnp.bfloat16)
    grad_up = (up_acc * mask_up.astype(jnp.float32)).astype(jnp.bfloat16)
    gate_rows = gate_grad
    up_rows = up_grad
    total = lax.dot_general(
        gate_rows, gate_masked, (((1,), (1,)), ((), ())), preferred_element_type=jnp.float32
    )
    grad_input = lax.psum_scatter(
        total
        + lax.dot_general(
            up_rows, up_masked, (((1,), (1,)), ((), ())), preferred_element_type=jnp.float32
        ),
        "tensor",
        scatter_dimension=0,
        tiled=True,
    ).astype(jnp.bfloat16)
    return (grad_input, grad_gate, grad_up, grad_down)


def solution(mesh):
    in_specs = (
        P("tensor", "pipe"),
        P("tensor", "pipe"),
        P(None, "tensor"),
        P(None, "tensor"),
        P("pipe", "tensor"),
        P("pipe", "tensor"),
        P("tensor", "pipe"),
        P("pipe", "tensor"),
        P("pipe", "tensor"),
        P("tensor", "pipe"),
    )
    out_specs = (P("tensor", "pipe"), P("pipe", "tensor"), P("pipe", "tensor"), P("tensor", "pipe"))
    return jax.shard_map(shards, mesh=mesh, in_specs=in_specs, out_specs=out_specs, check_vma=False)
```

profile of v0, /device:TPU:0, one launch (start us, length us, event | category | flops | bytes accessed | tf_op | source)
XLA Modules:
  0.0 404.0 jit_solution(1261620353858778361)
XLA Ops:
  7.2 0.7 all-gather.3.cloned.1.call-update
  7.9 0.8 fusion.17
  8.8 36.6 %all-gather.3.cloned.1.call-done = bf16[768,1024]{1,0:T(8,128)(2,1)} async-done(((bf16[48,1024]{1,0:T(8,128)(2,1)}), bf16[768,1024]{1,0:T(8,128)(2,1)}) %all-gather.3.cloned.1.call-update) | async-done | bytes 1572880 | tf_op jit(solution)/shard_map/all_gather | solution.py:43
  45.4 5.1 %broadcast_in_dim.31 = bf16[1792,8,128]{2,1,0:T(8,128)(2,1)S(1)} broadcast(bf16[1792,8]{1,0:T(8,128)(2,1)S(1)} %bitcast.66), dimensions={0,1} | broadcast | bytes 3698688 | tf_op jit(solution)/shard_map/broadcast_in_dim | solution.py:10
  50.6 6.4 %convolution_bitcast_fusion = f32[768,1792]{0,1:T(8,128)} fusion(bf16[768,1024]{1,0:T(8,128)(2,1)} %all-gather.3.cloned.1.call-done, bf16[1792,1024]{1,0:T(8,128)(2,1)S(1)} %copy-done.9, bf16[224,8,8,128]{3,2,1,0:T(8,128)(2,1)S(1)} %bitcast.64), kind=kOutput, calls=%fused_computation.22 | convolution fusion | flops 2820407296 | bytes 14417920 | tf_op jit(solution)/shard_map/dot_general | solution.py:47
  57.0 0.7 all-gather.5.cloned.1.call-update
  57.7 0.2 reduce-scatter.2.cloned.1.call-start
  58.0 3.3 copy.23
  61.3 4.5 %copy.24 = bf16[768,1792]{0,1:T(8,128)(2,1)} copy(bf16[768,1792]{1,0:T(8,128)(2,1)} %param.12) | data formatting | bytes 5505024 | tf_op args[2]
  65.8 0.1 copy.25
  65.9 0.1 broadcast_bitcast_fusion.3
  66.0 6.0 %copy.26 = bf16[1024,1792]{0,1:T(8,128)(2,1)} copy(bf16[1024,1792]{1,0:T(8,128)(2,1)} %param.14) | data formatting | bytes 7340032 | tf_op args[4]
  72.0 0.1 copy.27
  72.1 0.1 broadcast_bitcast_fusion.2
  72.3 6.0 %copy.28 = bf16[1024,1792]{0,1:T(8,128)(2,1)} copy(bf16[1024,1792]{1,0:T(8,128)(2,1)} %param.15) | data formatting | bytes 7340032 | tf_op args[5]
  78.2 4.3 %bitcast_multiply_fusion.6 = bf16[1024,1792]{0,1:T(8,128)(2,1)} fusion(bf16[1024,1792]{0,1:T(8,128)(2,1)} %copy.26, bf16[1024,14]{0,1:T(8,128)(2,1)S(1)} %bitcast.69), kind=kLoop, calls=%fused_computation.26 | loop fusion | flops 1835008 | bytes 7368704 | tf_op jit(solution)/shard_map/mul | solution.py:36
  82.5 2.1 bitcast_multiply_fusion.5
  84.6 207.2 %all-reduce.2.cloned.1.call-done = f32[768,1792]{0,1:T(8,128)} async-done(((f32[768,1792]{0,1:T(8,128)}), f32[768,1792]{0,1:T(8,128)}) %all-reduce.2.cloned.1.call-update) | async-done | bytes 5505040 | tf_op jit(solution)/shard_map/psum | solution.py:53
  291.8 5.0 %fusion.12 = (bf16[768,1792]{0,1:T(8,128)(2,1)S(1)}, bf16[768,1792]{0,1:T(8,128)(2,1)S(1)}) fusion(f32[768,1792]{0,1:T(8,128)} %all-reduce.2.cloned.1.call-done, bf16[768,1792]{0,1:T(8,128)(2,1)} %copy.24, bf16[768,1792]{0,1:T(8,128)(2,1)S(1)} %copy.23), kind=kLoop, calls=%fused_computation.21 | loop fusion | flops 20643840 | bytes 16515072 | tf_op jit(solution)/shard_map/convert_element_type | solution.py:17
  296.9 3.1 fusion.20
  300.0 0.9 copy-done.1
  300.9 4.9 %convolution_add_fusion = f32[768,1024]{1,0:T(8,128)} fusion(f32[768,1024]{1,0:T(8,128)S(1)} %fusion.20, bf16[768,1792]{0,1:T(8,128)(2,1)S(1)} %get-tuple-element.12, bf16[1024,1792]{0,1:T(8,128)(2,1)S(1)} %copy-done.1), kind=kOutput, calls=%fused_computation.28 | convolution fusion | flops 2819358720 | bytes 12713984 | tf_op jit(solution)/shard_map/dot_general | solution.py:74
  306.4 2.0 broadcast_in_dim.41
  308.5 0.2 copy-done.10
  308.7 5.2 %fusion = bf16[1792,1024]{1,0:T(8,128)(2,1)} fusion(f32[224,8,8,128]{3,2,1,0:T(8,128)S(1)} %bitcast.63, bf16[768,1024]{1,0:T(8,128)(2,1)S(1)} %copy-done.10, bf16[768,1792]{0,1:T(8,128)(2,1)S(1)} %copy.23, bf16[768,1792]{0,1:T(8,128)(2,1)S(1)} %copy-done.2), kind=kOutput, calls=%fused_computation.5 | convolution fusion | flops 2833252352 | bytes 18087936 | tf_op jit(solution)/shard_map/dot_general | solution.py:44
  313.9 14.5 %all-gather.5.cloned.1.call-done = bf16[768,1024]{1,0:T(8,128)(2,1)} async-done(((bf16[48,1024]{1,0:T(8,128)(2,1)}), bf16[768,1024]{1,0:T(8,128)(2,1)}) %all-gather.5.cloned.1.call-update) | async-done | bytes 1572880 | tf_op jit(solution)/shard_map/all_gather | solution.py:55
  328.4 7.1 %fusion.2 = bf16[1024,1792]{0,1:T(8,128)(2,1)} fusion(bf16[768,1792]{0,1:T(8,128)(2,1)} %copy-done.6, bf16[768,1024]{1,0:T(8,128)(2,1)} %all-gather.5.cloned.1.call-done, f32[1024,14]{0,1:T(8,128)S(1)} %bitcast.73), kind=kOutput, calls=%fused_computation.9 | convolution fusion | flops 2822242304 | bytes 8052736 | tf_op jit(solution)/shard_map/dot_general | solution.py:58
  335.5 6.1 %copy.32 = bf16[1024,1792]{1,0:T(8,128)(2,1)} copy(bf16[1024,1792]{0,1:T(8,128)(2,1)} %fusion.2) | data formatting | bytes 7340032
  341.6 6.2 %fusion.1 = bf16[1024,1792]{0,1:T(8,128)(2,1)} fusion(bf16[768,1792]{0,1:T(8,128)(2,1)S(1)} %copy-done.4, bf16[768,1024]{1,0:T(8,128)(2,1)} %all-gather.5.cloned.1.call-done, f32[1024,14]{0,1:T(8,128)S(1)} %bitcast.74), kind=kOutput, calls=%fused_computation.7 | convolution fusion | flops 2822242304 | bytes 8052736 | tf_op jit(solution)/shard_map/dot_general | solution.py:61
  347.8 5.9 %copy.33 = bf16[1024,1792]{1,0:T(8,128)(2,1)} copy(bf16[1024,1792]{0,1:T(8,128)(2,1)} %fusion.1) | data formatting | bytes 7340032
  353.7 42.1 %reduce-scatter.2.cloned.1.call-done = f32[48,1024]{1,0:T(8,128)} async-done(((f32[768,1024]{1,0:T(8,128)}), f32[48,1024]{1,0:T(8,128)}) %reduce-scatter.2.cloned.1.call-update) | async-done | bytes 196624 | tf_op jit(solution)/shard_map/reduce_scatter | solution.py:72
  395.9 1.6 convert_element_type.106
  (43 shorter events, 0.9 us)
Async XLA Ops:
  7.2 38.2 %all-gather.3.cloned.1.call-start = ((), (), s32[]{:S(2)}) async-start(), calls=%async_computation.1 | async-start | bytes 1671168 | tf_op jit(solution)/shard_map/all_gather | solution.py:43
  7.9 283.9 %all-reduce.2.cloned.1.call-start = ((), (), s32[]{:S(2)}) async-start(), calls=%async_computation.2 | async-start | bytes 11010048 | tf_op jit(solution)/shard_map/psum | solution.py:53
  45.4 5.2 %copy-start.9 = (bf16[1792,1024]{1,0:T(8,128)(2,1)S(1)}, bf16[1792,1024]{1,0:T(8,128)(2,1)}, u32[]{:S(2)}) copy-start(bf16[1792,1024]{1,0:T(8,128)(2,1)} %param.16) | copy-start | bytes 11010052
  57.0 271.4 %all-gather.5.cloned.1.call-start = ((), (), s32[]{:S(2)}) async-start(), calls=%async_computation.4 | async-start | bytes 1671168 | tf_op jit(solution)/shard_map/all_gather | solution.py:55
  57.7 338.2 %reduce-scatter.2.cloned.1.call-start = ((), (), s32[]{:S(2)}) async-start(), calls=%async_computation.3 | async-start | bytes 3342336 | tf_op jit(solution)/shard_map/reduce_scatter | solution.py:72
  61.3 4.5 %copy-start.7 = (s32[8,14]{1,0:T(8,128)S(1)}, s32[8,14]{1,0:T(8,128)}, u32[]{:S(2)}) copy-start(s32[8,14]{1,0:T(8,128)} %param.17) | copy-start | bytes 1348
  66.0 6.0 %copy-start.8 = (s32[8,14]{1,0:T(8,128)S(1)}, s32[8,14]{1,0:T(8,128)}, u32[]{:S(2)}) copy-start(s32[8,14]{1,0:T(8,128)} %param.18) | copy-start | bytes 1348
  78.2 4.3 %copy-start = (bf16[1024,1792]{0,1:T(8,128)(2,1)S(1)}, bf16[1024,1792]{0,1:T(8,128)(2,1)}, u32[]{:S(2)}) copy-start(bf16[1024,1792]{0,1:T(8,128)(2,1)} %copy.28) | copy-start | bytes 11010052
  291.8 5.1 %copy-start.5 = (bf16[1024,1792]{0,1:T(8,128)(2,1)S(1)}, bf16[1024,1792]{0,1:T(8,128)(2,1)}, u32[]{:S(2)}) copy-start(bf16[1024,1792]{0,1:T(8,128)(2,1)} %bitcast_multiply_fusion.6) | copy-start | bytes 11010052
  296.8 3.1 copy-start.6
  296.9 3.1 copy-start.3
  296.9 4.0 copy-start.1
  306.4 2.1 copy-start.2
  306.4 2.3 copy-start.10
  335.5 6.1 %copy-start.4 = (bf16[768,1792]{0,1:T(8,128)(2,1)S(1)}, bf16[768,1792]{0,1:T(8,128)(2,1)}, u32[]{:S(2)}) copy-start(bf16[768,1792]{0,1:T(8,128)(2,1)} %copy-done.3) | copy-start | bytes 8257540
Sparse Core Ops, SparseCore 0:
  9.7 35.6 all-gather.2
  57.1 234.6 all-reduce.1
  293.5 34.8 all-gather.4
  330.7 65.1 reduce-scatter.1
where the time goes:
time: 405 us; the launch traced here: 404 us
  waiting for transfers between devices  302 us (75%)
  local copies, waits for them, and re-layouts  41.1 us (10%)
  matrix products  32.9 us (8%)
  between operations  14 us (3%)
  other arithmetic  13.7 us (3%)
    psum x1, waiting for transfers between devices, shards(): hidden_grad = lax.psum(hidden_partial, 'pipe')  207 us
    reduce_scatter x1, waiting for transfers between devices, shards(): lax.psum_scatter(total + lax.dot_general(up_rows, up_masked, (((1,), (1,)...  42.1 us
    all_gather x1, waiting for transfers between devices, shards(): piece = lax.all_gather(out_grad, 'tensor', axis=0, tiled=True)  36.6 us
    unnamed x40, local copies, waits for them, and re-layouts  33.3 us
    all_gather x1, waiting for transfers between devices, shards(): piece = lax.all_gather(layer_input, 'tensor', axis=0, tiled=True)  14.5 us
  transfers between devices with their start and end apart: 4, of which 4 were waited for; matrix products, arithmetic and copies ran while one was open for 18% of the time, Pallas kernels for 0%

commit v1 on v0

--- a/solution.py
+++ b/solution.py
@@ -50,7 +50,8 @@
     hidden_grad = partial_rows
     down_acc, hidden_partial = (down_acc, hidden_grad)
     grad_down = (down_acc * mask_down.astype(jnp.float32)).astype(jnp.bfloat16)
-    hidden_grad = lax.psum(hidden_partial, "pipe")
+    parts = lax.all_gather(hidden_partial, "pipe")
+    hidden_grad = jnp.sum(parts, axis=0)
     gate_grad, up_grad = local_grads(hidden_grad, gate_val, up_val, sigma_val)
     piece = lax.all_gather(layer_input, "tensor", axis=0, tiled=True)
     gate_rows = gate_grad

time: 405 us -> 634 us (1.57)
  waiting for transfers between devices: 302 us -> 477 us
  local copies, waits for them, and re-layouts: 41.1 us -> 77.9 us
  other arithmetic: 13.7 us -> 31.4 us
    all_gather x0 -> x1, waiting for transfers between devices: none -> 409 us  [shards(): parts = lax.all_gather(hidden_partial, 'pipe')]
    psum x1 -> x0, waiting for transfers between devices: 207 us -> none  [shards(): hidden_grad = lax.psum(hidden_partial, 'pipe')]
    unnamed x40 -> x41, local copies, waits for them, and re-layouts: 33.3 us -> 69.8 us
    reduce_sum x0 -> x1, other arithmetic: none -> 17.6 us  [shards(): hidden_grad = jnp.sum(parts, axis=0)]
    all_gather x1, waiting for transfers between devices: 14.5 us -> 0.01 us  [shards(): piece = lax.all_gather(layer_input, 'tensor', axis=0, tiled=True)]
    reduce_scatter x1, waiting for transfers between devices: 42.1 us -> 29.6 us  [shards(): lax.psum_scatter(total + lax.dot_general(up_rows, up_masked, (((1,), (1,)...]
  transfers between devices with their start and end apart: 4 -> 4, of which waited for: 4 -> 3; matrix products, arithmetic and copies ran while one was open for 18% -> 20% of each run, Pallas kernels for 0% -> 0%
where the time goes in v1:
time: 634 us; the launch traced here: 633 us
  waiting for transfers between devices  477 us (75%)
  local copies, waits for them, and re-layouts  77.9 us (12%)
  matrix products  32.9 us (5%)
  other arithmetic  31.4 us (5%)
  between operations  14 us (2%)
    all_gather x1, waiting for transfers between devices, shards(): parts = lax.all_gather(hidden_partial, 'pipe')  409 us
    unnamed x41, local copies, waits for them, and re-layouts  69.8 us
    all_gather x1, waiting for transfers between devices, shards(): piece = lax.all_gather(out_grad, 'tensor', axis=0, tiled=True)  36.6 us
    reduce_scatter x1, waiting for transfers between devices, shards(): lax.psum_scatter(total + lax.dot_general(up_rows, up_masked, (((1,), (1,)...  29.6 us
    reduce_sum x1, other arithmetic, shards(): hidden_grad = jnp.sum(parts, axis=0)  17.6 us
  transfers between devices with their start and end apart: 4, of which 3 were waited for; matrix products, arithmetic and copies ran while one was open for 20% of the time, Pallas kernels for 0%

profile of v1, /device:TPU:0, one launch (start us, length us, event | category | flops | bytes accessed | tf_op | source)
XLA Modules:
  0.0 633.0 jit_solution(15458881887943194331)
XLA Ops:
  7.2 0.7 all-gather.5.cloned.1.call-update
  7.9 0.8 fusion.17
  8.8 36.6 %all-gather.5.cloned.1.call-done = bf16[768,1024]{1,0:T(8,128)(2,1)} async-done(((bf16[48,1024]{1,0:T(8,128)(2,1)}), bf16[768,1024]{1,0:T(8,128)(2,1)}) %all-gather.5.cloned.1.call-update) | async-done | bytes 1572880 | tf_op jit(solution)/shard_map/all_gather | solution.py:43
  45.4 5.1 broadcast_in_dim.31
  50.6 6.3 convolution_bitcast_fusion
  56.9 0.7 all-gather.7.cloned.1.call-update
  57.6 0.2 reduce-scatter.2.cloned.1.call-start
  57.8 3.3 copy.31
  61.2 4.5 copy.32
  65.7 0.1 copy.33
  65.8 0.1 broadcast_bitcast_fusion.3
  65.9 6.5 %copy.34 = bf16[1024,1792]{0,1:T(8,128)(2,1)} copy(bf16[1024,1792]{1,0:T(8,128)(2,1)} %param.14) | data formatting | bytes 7340032 | tf_op args[4]
  72.5 0.1 copy.35
  72.6 0.1 broadcast_bitcast_fusion.2
  72.7 6.1 copy.36
  78.8 4.3 bitcast_multiply_fusion.6
  83.1 2.1 bitcast_multiply_fusion.5
  85.2 409.1 %all-gather.9.cloned.1.call-done = f32[6144,1792]{0,1:T(8,128)} async-done(((f32[768,1792]{0,1:T(8,128)}), f32[6144,1792]{0,1:T(8,128)}) %all-gather.9.cloned.1.call-update) | async-done | bytes 44040208 | tf_op jit(solution)/shard_map/all_gather | solution.py:53
  494.2 36.0 %copy.43 = f32[224,8,8,768]{3,2,1,0:T(8,128)} copy(f32[224,8,8,768]{3,1,2,0:T(8,128)} %bitcast.68) | data formatting | bytes 88080384
  530.3 17.6 %bitcast_reduce_fusion = f32[768,1792]{0,1:T(8,128)} fusion(f32[224,8,8,768]{3,2,1,0:T(8,128)} %copy.43), kind=kLoop, calls=%fused_computation | loop fusion | flops 9633792 | bytes 49545216 | tf_op jit(solution)/shard_map/reduce_sum | solution.py:54
  547.9 5.0 fusion.12
  553.0 3.1 fusion.20
  556.1 0.9 copy-done.1
  557.0 4.9 convolution_add_fusion
  562.5 2.3 broadcast_in_dim.41
  564.8 5.2 fusion
  570.0 7.1 %fusion.2 = bf16[1024,1792]{0,1:T(8,128)(2,1)} fusion(bf16[768,1792]{0,1:T(8,128)(2,1)} %copy-done.6, bf16[768,1024]{1,0:T(8,128)(2,1)} %all-gather.7.cloned.1.call-done, f32[1024,14]{0,1:T(8,128)S(1)} %bitcast.79), kind=kOutput, calls=%fused_computation.10 | convolution fusion | flops 2822242304 | bytes 8052736 | tf_op jit(solution)/shard_map/dot_general | solution.py:59
  577.1 6.1 copy.40
  583.2 6.2 fusion.1
  589.4 5.9 copy.41
  595.3 29.6 %reduce-scatter.2.cloned.1.call-done = f32[48,1024]{1,0:T(8,128)} async-done(((f32[768,1024]{1,0:T(8,128)}), f32[48,1024]{1,0:T(8,128)}) %reduce-scatter.2.cloned.1.call-update) | async-done | bytes 196624 | tf_op jit(solution)/shard_map/reduce_scatter | solution.py:73
  624.9 1.6 convert_element_type.106
  (45 shorter events, 0.9 us)
Async XLA Ops:
  7.2 38.2 %all-gather.5.cloned.1.call-start = ((), (), s32[]{:S(2)}) async-start(), calls=%async_computation.1 | async-start | bytes 1671168 | tf_op jit(solution)/shard_map/all_gather | solution.py:43
  7.9 486.3 %all-gather.9.cloned.1.call-start = ((), (), s32[]{:S(2)}) async-start(), calls=%async_computation.4 | async-start | bytes 49545216 | tf_op jit(solution)/shard_map/all_gather | solution.py:53
  45.4 5.2 copy-start.9
  56.9 513.1 %all-gather.7.cloned.1.call-start = ((), (), s32[]{:S(2)}) async-start(), calls=%async_computation.3 | async-start | bytes 1671168 | tf_op jit(solution)/shard_map/all_gather | solution.py:56
  57.6 567.3 %reduce-scatter.2.cloned.1.call-start = ((), (), s32[]{:S(2)}) async-start(), calls=%async_computation.2 | async-start | bytes 3342336 | tf_op jit(solution)/shard_map/reduce_scatter | solution.py:73
  61.2 4.5 copy-start.7
  65.9 6.5 %copy-start.8 = (s32[8,14]{1,0:T(8,128)S(1)}, s32[8,14]{1,0:T(8,128)}, u32[]{:S(2)}) copy-start(s32[8,14]{1,0:T(8,128)} %param.18) | copy-start | bytes 1348
  78.8 4.3 copy-start
  547.9 5.1 copy-start.5
  552.9 3.1 copy-start.6
  552.9 3.1 copy-start.3
  553.0 4.0 copy-start.1
  562.5 2.3 copy-start.2
  562.5 2.3 copy-start.10
  577.1 6.1 copy-start.4
Sparse Core Ops, SparseCore 0:
  9.7 35.6 all-gather.4
  57.0 437.1 all-gather.8
  495.9 30.8 all-gather.6
  562.1 62.8 reduce-scatter.1
